TPU v7x, 32 devices: a whole 2x2x4 slice. The times are simulated.
32 devices in a mesh: train: 8 (over z, core), query: 4 (over y, x).
Axes of the slice: x: 2, y: 2, z: 4, core: 2. Of those that a mesh axis runs over, the one named last changes fastest.
Arguments:
- train_losses: float32 [256, 65536], P('train', 'query'), may hold values from 0 to 16
- query_losses: float32 [256, 8192], P('train', 'query'), may hold values from 0 to 16
- chain_slots: int32 [32], replicated, may hold values from 0 to 31, as said below
- doc_lengths: int32 [64], replicated, may hold values from 1 to 4096, 65536 in all
Outputs:
- influence: float32 [64, 8192], P('train', 'query')
Inputs may be any that keep to these rules, and one draw needn't show every extreme that they name: `chain_slots`: every chain appears exactly once. `doc_lengths`: the documents cover all 65536 train tokens in order.
All inputs are finite; a program needn't handle non-finite values.
Results may differ from a plain program's by a relative error of at most 0.00084.
Values may be sent and summed in bfloat16 or wider, within the bound.
A program may use at most 64 MiB of HBM per device.

v0:
```python
import jax
import jax.numpy as jnp
from jax import lax
from jax.sharding import PartitionSpec as P

DRAWS = 256
CHAINS = 32


epsilon = 1e-06
highest = lax.Precision.HIGHEST


def row_scale(centered):
    widened = centered.astype(jnp.float32)
    return lax.rsqrt(jnp.sum(widened * widened, axis=0) / (centered.shape[0] - 1) + epsilon)


def deal_columns(block, groups):
    height = block.shape[0]
    width = block.shape[1]
    return block.reshape(height, width // groups, groups).transpose(0, 2, 1).reshape(height, width)


def accumulate(running, centered, positions, query_paired, query_weights, doc_starts, doc_ends):
    row_total = centered.shape[1]
    block_size = min(1024, row_total)
    full_blocks = row_total // block_size

    def add_piece(running_sum, portion, places):
        scales = row_scale(portion)
        covariance = lax.dot_general(
            portion, query_paired, (((0,), (0,)), ((), ())), preferred_element_type=jnp.float32
        )
        correlation = covariance * scales[:, None] * query_weights[None, :] / (DRAWS - 1)
        signed = correlation * jnp.abs(correlation)
        inside = (places[:, None] >= doc_starts[None, :]) & (places[:, None] < doc_ends[None, :])
        member = inside.astype(jnp.float32)
        return running_sum + lax.dot_general(
            member,
            signed,
            (((0,), (0,)), ((), ())),
            precision=highest,
            preferred_element_type=jnp.float32,
        )

    def add_block(block_index, running_sum):
        offset = block_index * block_size
        portion = lax.dynamic_slice_in_dim(centered, offset, block_size, 1)
        places = lax.dynamic_slice_in_dim(positions, offset, block_size, 0)
        return add_piece(running_sum, portion, places)

    running = lax.fori_loop(0, full_blocks, add_block, running)
    return running


def shards(train_losses, query_losses, chain_slots, doc_lengths):
    train_parts = lax.axis_size("train")
    train_rank = lax.axis_index("train")
    tokens_here = train_losses.shape[1]
    piece_rows = tokens_here // train_parts
    query_whole = lax.all_gather(query_losses, "train", axis=0, tiled=True)
    columns_here = query_whole.shape[1]
    query_centered = (query_whole - jnp.sum(query_whole, axis=0)[None, :] / DRAWS).astype(
        jnp.bfloat16
    )
    query_paired = jnp.take(
        query_centered.reshape(CHAINS, DRAWS // CHAINS, columns_here), chain_slots, axis=0
    ).reshape(DRAWS, columns_here)
    query_weights = row_scale(query_paired)
    doc_ends = jnp.cumsum(doc_lengths)
    doc_starts = doc_ends - doc_lengths
    doc_total = doc_lengths.shape[0]
    docs_here = doc_total // train_parts
    running = jnp.zeros((doc_total, columns_here), jnp.float32)
    arrived = lax.all_to_all(
        deal_columns(train_losses, train_parts), "train", split_axis=1, concat_axis=0, tiled=True
    )
    centered_here = (arrived - jnp.sum(arrived, axis=0)[None, :] / DRAWS).astype(jnp.bfloat16)
    portion = lax.all_gather(centered_here, "query", axis=1, tiled=True)
    span_rows = portion.shape[1]
    gathered_index = jnp.arange(span_rows, dtype=jnp.int32)
    places = (
        gathered_index // piece_rows * tokens_here
        + gathered_index % piece_rows * train_parts
        + train_rank
    )
    running = accumulate(
        running, portion, places, query_paired, query_weights, doc_starts, doc_ends
    )
    owned_docs = lax.psum_scatter(running, "train", scatter_dimension=0, tiled=True)
    lengths_here = lax.dynamic_slice_in_dim(
        doc_lengths, train_rank * docs_here, docs_here, 0
    ).astype(jnp.float32)
    return owned_docs / lengths_here[:, None]


def solution(mesh):
    in_specs = (P("train", "query"), P("train", "query"), P(), P())
    out_specs = P("train", "query")
    return jax.shard_map(shards, mesh=mesh, in_specs=in_specs, out_specs=out_specs, check_vma=False)
```

profile of v0, /device:TPU:0, one launch (start us, length us, event | category | flops | bytes accessed | tf_op | source)
XLA Modules:
  0.0 252.3 jit_solution(7570533998084370612)
XLA Ops:
  6.5 6.2 %copy.14 = f32[32,16384]{0,1:T(8,128)} copy(f32[32,16384]{1,0:T(8,128)} %param.6) | data formatting | bytes 4194304 | tf_op args[0]
  12.8 6.3 %copy.15 = f32[32,8,2048]{2,0,1:T(8,128)} copy(f32[32,8,2048]{0,1,2:T(8,128)} %bitcast.17) | data formatting | bytes 4194304 | tf_op jit(solution)/shard_map/transpose | solution.py:22
  19.1 6.4 %all-to-all-start = ((f32[32,8,2048]{2,0,1:T(8,128)}), f32[32,8,2048]{2,0,1:T(8,128)S(1)}, u32[]{:S(2)}, u32[]{:S(2)}) async-start(f32[32,8,2048]{2,0,1:T(8,128)} %copy.15), calls=%async_computation | async-start | bytes 4194304 | tf_op jit(solution)/shard_map/all_to_all | solution.py:76
  26.2 65.1 %all-to-all-done = f32[32,8,2048]{2,0,1:T(8,128)S(1)} async-done(((f32[32,8,2048]{2,0,1:T(8,128)}), f32[32,8,2048]{2,0,1:T(8,128)S(1)}, u32[]{:S(2)}, u32[]{:S(2)}) %all-to-all-start) | async-done | bytes 2097184 | tf_op jit(solution)/shard_map/all_to_all | solution.py:76
  95.1 1.8 fusion.19
  98.0 46.3 %all-gather.3.cloned.1.call-done = bf16[256,8192]{1,0:T(8,128)(2,1)} async-done(((bf16[256,2048]{1,0:T(8,128)(2,1)}), bf16[256,8192]{1,0:T(8,128)(2,1)}) %all-gather.3.cloned.1.call-update) | async-done | bytes 4194320 | tf_op jit(solution)/shard_map/all_gather | solution.py:80
  144.3 67.5 %while.14 = (s32[]{:T(128)}, f32[64,2048]{1,0:T(8,128)S(1)}, s32[8192]{0:T(1024)S(1)}, s32[64]{0:T(128)S(1)}, s32[64]{0:T(128)S(1)}, /*index=5*/bf16[256,8192]{1...) while((s32[]{:T(128)}, f32[64,2048]{1,0:T(8,128)S(1)}, ...), condition=%wide.region_6.7_spmd.clone, body=%wide.region_4.6_spmd.clone.sunk | while | flops 2696086528 | bytes 19960512 | solution.py:53
  145.5 2.3 fusion.40
  147.9 4.9 %fusion.41 = f32[64,2048]{1,0:T(8,128)S(1)} fusion(f32[1024,2048]{1,0:T(8,128)S(1)} %fusion.40, f32[2048]{0:T(1024)S(1)} %get-tuple-element.268, f32[1024]{0:T(1024)S(1)} %add_rsqrt_fusion.3, f32[64,2048]{1,0:T(8,128)S(1)} %get-tuple-element.250, s32[64]{0:T(128)S(1)} %get-tuple-element.265, s32[64]{0:T(128)S(1)} %get-tuple-element.264, ...), kind=kOutput, calls=%fused_computation.9.clone.1 | convolution fusion | flops 1621557248 | bytes 9454081 | tf_op jit(solution)/shard_map/while/body/eval_jaxpr/dot_general | solution.py:39
  154.0 2.3 fusion.40
  156.3 4.9 %fusion.41 = f32[64,2048]{1,0:T(8,128)S(1)} fusion(f32[1024,2048]{1,0:T(8,128)S(1)} %fusion.40, f32[2048]{0:T(1024)S(1)} %get-tuple-element.268, f32[1024]{0:T(1024)S(1)} %add_rsqrt_fusion.3, f32[64,2048]{1,0:T(8,128)S(1)} %get-tuple-element.250, s32[64]{0:T(128)S(1)} %get-tuple-element.265, s32[64]{0:T(128)S(1)} %get-tuple-element.264, ...), kind=kOutput, calls=%fused_computation.9.clone.1 | convolution fusion | flops 1621557248 | bytes 9454081 | tf_op jit(solution)/shard_map/while/body/eval_jaxpr/dot_general | solution.py:39
  162.4 2.3 fusion.40
  164.7 4.9 %fusion.41 = f32[64,2048]{1,0:T(8,128)S(1)} fusion(f32[1024,2048]{1,0:T(8,128)S(1)} %fusion.40, f32[2048]{0:T(1024)S(1)} %get-tuple-element.268, f32[1024]{0:T(1024)S(1)} %add_rsqrt_fusion.3, f32[64,2048]{1,0:T(8,128)S(1)} %get-tuple-element.250, s32[64]{0:T(128)S(1)} %get-tuple-element.265, s32[64]{0:T(128)S(1)} %get-tuple-element.264, ...), kind=kOutput, calls=%fused_computation.9.clone.1 | convolution fusion | flops 1621557248 | bytes 9454081 | tf_op jit(solution)/shard_map/while/body/eval_jaxpr/dot_general | solution.py:39
  170.8 2.3 fusion.40
  173.2 4.9 %fusion.41 = f32[64,2048]{1,0:T(8,128)S(1)} fusion(f32[1024,2048]{1,0:T(8,128)S(1)} %fusion.40, f32[2048]{0:T(1024)S(1)} %get-tuple-element.268, f32[1024]{0:T(1024)S(1)} %add_rsqrt_fusion.3, f32[64,2048]{1,0:T(8,128)S(1)} %get-tuple-element.250, s32[64]{0:T(128)S(1)} %get-tuple-element.265, s32[64]{0:T(128)S(1)} %get-tuple-element.264, ...), kind=kOutput, calls=%fused_computation.9.clone.1 | convolution fusion | flops 1621557248 | bytes 9454081 | tf_op jit(solution)/shard_map/while/body/eval_jaxpr/dot_general | solution.py:39
  179.3 2.3 fusion.40
  181.6 4.9 %fusion.41 = f32[64,2048]{1,0:T(8,128)S(1)} fusion(f32[1024,2048]{1,0:T(8,128)S(1)} %fusion.40, f32[2048]{0:T(1024)S(1)} %get-tuple-element.268, f32[1024]{0:T(1024)S(1)} %add_rsqrt_fusion.3, f32[64,2048]{1,0:T(8,128)S(1)} %get-tuple-element.250, s32[64]{0:T(128)S(1)} %get-tuple-element.265, s32[64]{0:T(128)S(1)} %get-tuple-element.264, ...), kind=kOutput, calls=%fused_computation.9.clone.1 | convolution fusion | flops 1621557248 | bytes 9454081 | tf_op jit(solution)/shard_map/while/body/eval_jaxpr/dot_general | solution.py:39
  187.7 2.3 fusion.40
  190.0 4.9 %fusion.41 = f32[64,2048]{1,0:T(8,128)S(1)} fusion(f32[1024,2048]{1,0:T(8,128)S(1)} %fusion.40, f32[2048]{0:T(1024)S(1)} %get-tuple-element.268, f32[1024]{0:T(1024)S(1)} %add_rsqrt_fusion.3, f32[64,2048]{1,0:T(8,128)S(1)} %get-tuple-element.250, s32[64]{0:T(128)S(1)} %get-tuple-element.265, s32[64]{0:T(128)S(1)} %get-tuple-element.264, ...), kind=kOutput, calls=%fused_computation.9.clone.1 | convolution fusion | flops 1621557248 | bytes 9454081 | tf_op jit(solution)/shard_map/while/body/eval_jaxpr/dot_general | solution.py:39
  196.1 2.3 fusion.40
  198.5 4.9 %fusion.41 = f32[64,2048]{1,0:T(8,128)S(1)} fusion(f32[1024,2048]{1,0:T(8,128)S(1)} %fusion.40, f32[2048]{0:T(1024)S(1)} %get-tuple-element.268, f32[1024]{0:T(1024)S(1)} %add_rsqrt_fusion.3, f32[64,2048]{1,0:T(8,128)S(1)} %get-tuple-element.250, s32[64]{0:T(128)S(1)} %get-tuple-element.265, s32[64]{0:T(128)S(1)} %get-tuple-element.264, ...), kind=kOutput, calls=%fused_computation.9.clone.1 | convolution fusion | flops 1621557248 | bytes 9454081 | tf_op jit(solution)/shard_map/while/body/eval_jaxpr/dot_general | solution.py:39
  204.6 2.3 fusion.40
  206.9 4.9 %fusion.41 = f32[64,2048]{1,0:T(8,128)S(1)} fusion(f32[1024,2048]{1,0:T(8,128)S(1)} %fusion.40, f32[2048]{0:T(1024)S(1)} %get-tuple-element.268, f32[1024]{0:T(1024)S(1)} %add_rsqrt_fusion.3, f32[64,2048]{1,0:T(8,128)S(1)} %get-tuple-element.250, s32[64]{0:T(128)S(1)} %get-tuple-element.265, s32[64]{0:T(128)S(1)} %get-tuple-element.264, ...), kind=kOutput, calls=%fused_computation.9.clone.1 | convolution fusion | flops 1621557248 | bytes 9454081 | tf_op jit(solution)/shard_map/while/body/eval_jaxpr/dot_general | solution.py:39
  212.7 31.5 %reduce-scatter.2.cloned.1.call-done = f32[8,2048]{1,0:T(8,128)} async-done(((f32[64,2048]{1,0:T(8,128)}), f32[8,2048]{1,0:T(8,128)}) %reduce-scatter.2.cloned.1.call-update) | async-done | bytes 65552 | tf_op jit(solution)/shard_map/reduce_scatter | solution.py:91
  (59 shorter events, 17.5 us)
Async XLA Ops:
  19.1 72.2 %all-to-all-start = ((f32[32,8,2048]{2,0,1:T(8,128)}), f32[32,8,2048]{2,0,1:T(8,128)S(1)}, u32[]{:S(2)}, u32[]{:S(2)}) async-start(f32[32,8,2048]{2,0,1:T(8,128)} %copy.15), calls=%async_computation | async-start | bytes 4194304 | tf_op jit(solution)/shard_map/all_to_all | solution.py:76
  25.4 67.3 %copy-start.2 = (s32[32]{0:T(128)S(1)}, s32[32]{0:T(128)}, u32[]{:S(2)}) copy-start(s32[32]{0:T(128)} %param.8) | copy-start | bytes 388
  25.4 67.5 %copy-start.1 = (s32[64]{0:T(128)S(1)}, s32[64]{0:T(128)}, u32[]{:S(2)}) copy-start(s32[64]{0:T(128)} %param.9) | copy-start | bytes 772
  25.5 67.9 %all-gather.5.cloned.1.call-start = ((), (), s32[]{:S(2)}) async-start(), calls=%async_computation.3 | async-start | bytes 2359296 | tf_op jit(solution)/shard_map/all_gather | solution.py:62
  26.2 118.1 %all-gather.3.cloned.1.call-start = ((), (), s32[]{:S(2)}) async-start(), calls=%async_computation.2 | async-start | bytes 5242880 | tf_op jit(solution)/shard_map/all_gather | solution.py:80
  92.7 151.5 %reduce-scatter.2.cloned.1.call-start = ((), (), s32[]{:S(2)}) async-start(), calls=%async_computation.4 | async-start | bytes 589824 | tf_op jit(solution)/shard_map/reduce_scatter | solution.py:91
  211.8 0.8 copy-start
Sparse Core Ops, SparseCore 0:
  27.9 57.1 all-gather.4
  92.8 51.4 all-gather.2
  212.7 31.3 reduce-scatter.1
where the time goes:
time: 253 us; the launch traced here: 252 us
  waiting for transfers between devices  144 us (57%)
  matrix products  57.6 us (23%)
  other arithmetic  16.6 us (7%)
  local copies, waits for them, and re-layouts  14.3 us (6%)
  between operations  13.3 us (5%)
  starting transfers between devices  6.48 us (3%)
    all_to_all x1, waiting for transfers between devices, shards(): lax.all_to_all(deal_columns(train_losses, train_parts), 'train', split_ax...  65.1 us
    all_gather x1, waiting for transfers between devices, shards(): portion = lax.all_gather(centered_here, 'query', axis=1, tiled=True)  46.3 us
    dot_general x8, matrix products, add_piece(): lax.dot_general(member, signed, (((0,), (0,)), ((), ())), precision=highe...  38.9 us
    reduce_scatter x1, waiting for transfers between devices, shards(): lax.psum_scatter(running, 'train', scatter_dimension=0, tiled=True)  31.5 us
    dot_general x8, matrix products, add_piece(): lax.dot_general(portion, query_paired, (((0,), (0,)), ((), ())), preferre...  18.7 us
    reduce_sum x9, other arithmetic, row_scale(): jnp.sum(widened * widened, axis=0) / (centered.shape[0] - 1) + epsilon  9.73 us
    unnamed x7, local copies, waits for them, and re-layouts  7.04 us
    all_to_all x1, starting transfers between devices, shards(): lax.all_to_all(deal_columns(train_losses, train_parts), 'train', split_ax...  6.35 us
  transfers between devices with their start and end apart: 4, of which 3 were waited for; matrix products, arithmetic and copies ran while one was open for 3% of the time, Pallas kernels for 0%

commit v1 on v0

v1 whole, which is shorter than its diff:
```python
import functools

import jax
import jax.numpy as jnp
from jax import lax
from jax.experimental import pallas as pl
from jax.experimental.pallas import tpu as pltpu
from jax.sharding import PartitionSpec as P

MESH = pl.DeviceIdType.MESH
epsilon = 1e-06
per_chain = 8


def remote(src, dst, send, recv, device):
    return pltpu.make_async_remote_copy(
        src_ref=src, dst_ref=dst, send_sem=send, recv_sem=recv, device_id=device, device_id_type=MESH
    )


def gather_kernel(
    n_t, n_q, x_ref, y_ref, g_ref, q_ref,
    sums, parts, means, cent, centq,
    s1, r1, s2, r2, sa, ra, sq, rq, sf, rf, sb, rb, sr, rr, s0, r0, sh, rh, local_sem,
):
    t = lax.axis_index("train")
    q = lax.axis_index("query")
    n_m, n_a = n_t // 2, n_q // 2
    m, c = t // 2, lax.rem(t, 2)
    sibling = 2 * m + 1 - c
    a, b = q // 2, lax.rem(q, 2)
    partner = 2 * a + 1 - b
    others = [lax.rem(a + k, n_a) for k in range(1, n_a)]
    columns = [2 * other + b for other in others]
    half = cent.shape[3]
    piece = 2 * half
    spread = y_ref.shape[1] // n_t
    draws = x_ref.shape[0] * n_t

    barrier = pltpu.get_barrier_semaphore()
    for k in range(1, n_t):
        pl.semaphore_signal(barrier, inc=1, device_id=(lax.rem(t + k, n_t), q), device_id_type=MESH)
    for target in [partner] + columns:
        pl.semaphore_signal(barrier, inc=1, device_id=(t, target), device_id_type=MESH)
    for r in range(n_t):
        sums[r, :, 0:piece] = jnp.sum(x_ref[:, r * piece:(r + 1) * piece], axis=0, keepdims=True)
        sums[r, :, piece:piece + spread] = jnp.sum(
            y_ref[:, r * spread:(r + 1) * spread], axis=0, keepdims=True
        )
    pl.semaphore_wait(barrier, n_t - 1 + n_a)

    sends, sources = [sibling], [sibling]
    for k in range(1, n_m):
        up, down = lax.rem(m + k, n_m), lax.rem(m + n_m - k, n_m)
        sends += [2 * up + c, 2 * up + 1 - c]
        sources += [2 * down + c, 2 * down + 1 - c]

    started = []
    for r in sends:
        copy = remote(sums.at[r], parts.at[t], s1.at[r], r1.at[t], (r, q))
        copy.start()
        started.append(copy)
    total = sums[t]
    for r in sources:
        remote(parts.at[r], parts.at[r], s1.at[r], r1.at[r], (r, q)).wait_recv()
        total = total + parts[r]
    means[t] = total / draws
    for r in sends:
        copy = remote(means.at[t], means.at[t], s2.at[r], r2.at[t], (r, q))
        copy.start()
        started.append(copy)

    def center(r):
        for h in range(2):
            begin = pl.multiple_of(r * piece + h * half, 128)
            cent[r, h] = (
                x_ref[:, pl.ds(begin, half)] - means[r, :, h * half:(h + 1) * half]
            ).astype(jnp.bfloat16)
        begin = pl.multiple_of(r * spread, 128)
        centq[:, pl.ds(begin, spread)] = (
            y_ref[:, pl.ds(begin, spread)] - means[r, :, piece:piece + spread]
        ).astype(jnp.bfloat16)

    def spread_block(src, tp):
        copy = remote(src, g_ref.at[q, :, tp], sb.at[tp], rb.at[tp], (t, partner))
        copy.start()
        started.append(copy)
        for k in range(n_a - 1):
            copy = remote(src, g_ref.at[q, :, tp], sr.at[tp, others[k]], rr.at[tp, a], (t, columns[k]))
            copy.start()
            started.append(copy)

    def pass_on(tp):
        whole = g_ref.at[partner, :, tp]
        remote(whole, whole, sb.at[tp], rb.at[tp], (t, partner)).wait_recv()
        for k in range(n_a - 1):
            first = g_ref.at[partner, 0, tp]
            copy = remote(first, first, s0.at[tp, others[k]], r0.at[tp, a], (t, columns[k]))
            copy.start()
            started.append(copy)
        for k in range(n_a - 1):
            whole = g_ref.at[columns[k], :, tp]
            remote(whole, whole, sr.at[tp, others[k]], rr.at[tp, others[k]], (t, columns[k])).wait_recv()
            second = g_ref.at[columns[k], 1, tp]
            copy = remote(second, second, sh.at[tp, others[k]], rh.at[tp, others[k]], (t, partner))
            copy.start()
            started.append(copy)

    center(t)
    spread_block(cent.at[t], t)
    own = pltpu.make_async_copy(cent.at[t], g_ref.at[q, :, t], local_sem.at[0])
    own.start()
    arrivals = [sibling]
    for k in range(1, n_m):
        down = lax.rem(m + n_m - k, n_m)
        arrivals += [2 * down + c, 2 * down + 1 - c]
    sent = [sends[i] for i in range(1, n_t - 1)] + [sends[0]]
    for r in sent:
        remote(means.at[r], means.at[r], s2.at[r], r2.at[r], (r, q)).wait_recv()
        center(r)
        copy = remote(cent.at[r], g_ref.at[q, :, t], sa.at[r], ra.at[t], (r, q))
        copy.start()
        started.append(copy)
    for k in range(1, n_m):
        up = lax.rem(m + k, n_m)
        copy = remote(centq, q_ref.at[t], sq.at[up], rq.at[m], (2 * up + c, q))
        copy.start()
        started.append(copy)
    copy = remote(centq, q_ref.at[t], sf.at[m], rf.at[m], (sibling, q))
    copy.start()
    started.append(copy)
    ownq = pltpu.make_async_copy(centq, q_ref.at[t], local_sem.at[1])
    ownq.start()

    before = t
    for tp in arrivals:
        block = g_ref.at[q, :, tp]
        remote(block, block, sa.at[tp], ra.at[tp], (tp, q)).wait_recv()
        spread_block(block, tp)
        pass_on(before)
        before = tp
    pass_on(before)
    for k in range(1, n_m):
        down = lax.rem(m + n_m - k, n_m)
        block = q_ref.at[2 * down + c]
        remote(block, block, sq.at[down], rq.at[down], (2 * down + c, q)).wait_recv()
        copy = remote(block, block, sf.at[down], rf.at[down], (sibling, q))
        copy.start()
        started.append(copy)
    for k in range(n_m):
        block = q_ref.at[2 * k + 1 - c]
        remote(block, block, sf.at[k], rf.at[k], (sibling, q)).wait_recv()
    for tp in [t] + arrivals:
        for k in range(n_a - 1):
            diagonal = 2 * others[k] + 1 - b
            first = g_ref.at[diagonal, 0, tp]
            remote(first, first, s0.at[tp, others[k]], r0.at[tp, others[k]], (t, columns[k])).wait_recv()
            second = g_ref.at[diagonal, 1, tp]
            remote(second, second, sh.at[tp, others[k]], rh.at[tp, others[k]], (t, partner)).wait_recv()
    for copy in started:
        copy.wait_send()
    own.wait()
    ownq.wait()


def gather(train_losses, query_losses, n_t, n_q):
    draws_here, tokens = train_losses.shape
    queries = query_losses.shape[1]
    half = tokens // n_t // 2
    width = 2 * half + queries // n_t
    n_m, n_a = n_t // 2, n_q // 2
    dma = pltpu.SemaphoreType.DMA
    bf16 = jnp.bfloat16
    return pl.pallas_call(
        functools.partial(gather_kernel, n_t, n_q),
        out_shape=(
            jax.ShapeDtypeStruct((n_q, 2, n_t, draws_here, half), bf16),
            jax.ShapeDtypeStruct((n_t, draws_here, queries), bf16),
        ),
        in_specs=[pl.BlockSpec(memory_space=pltpu.VMEM)] * 2,
        out_specs=[pl.BlockSpec(memory_space=pl.ANY)] * 2,
        scratch_shapes=[
            pltpu.VMEM((n_t, 1, width), jnp.float32),
            pltpu.VMEM((n_t, 1, width), jnp.float32),
            pltpu.VMEM((n_t, 1, width), jnp.float32),
            pltpu.VMEM((n_t, 2, draws_here, half), bf16),
            pltpu.VMEM((draws_here, queries), bf16),
            dma((n_t,)), dma((n_t,)), dma((n_t,)), dma((n_t,)), dma((n_t,)), dma((n_t,)),
            dma((n_m,)), dma((n_m,)), dma((n_m,)), dma((n_m,)),
            dma((n_t,)), dma((n_t,)),
            dma((n_t, n_a)), dma((n_t, n_a)), dma((n_t, n_a)), dma((n_t, n_a)),
            dma((n_t, n_a)), dma((n_t, n_a)),
            dma((2,)),
        ],
        compiler_params=pltpu.CompilerParams(
            collective_id=0, has_side_effects=True, vmem_limit_bytes=40 << 20
        ),
    )(train_losses, query_losses)


def pool_kernel(
    lengths, slots, rank, g_ref, q_ref, out_ref, wide, paired, acc, turned, weights, ends, *, tokens, piece
):
    step = pl.program_id(0)
    draws, half = g_ref.shape[1], g_ref.shape[2]
    docs, queries = out_ref.shape
    tile = min(256, half)
    strip = min(256, queries)

    @pl.when(step == 0)
    def _():
        wide[...] = q_ref[...].astype(jnp.float32)

        def pair(s, carry):
            first = pl.multiple_of(slots[2 * s] * per_chain, per_chain)
            second = pl.multiple_of(slots[2 * s + 1] * per_chain, per_chain)
            rows = jnp.concatenate(
                [wide[pl.ds(first, per_chain), :], wide[pl.ds(second, per_chain), :]], axis=0
            )
            target = pl.multiple_of(s * 2 * per_chain, 2 * per_chain)
            paired[pl.ds(target, 2 * per_chain), :] = rows.astype(jnp.bfloat16)
            return carry

        lax.fori_loop(0, draws // per_chain // 2, pair, 0)

        def end(k, total):
            total = total + lengths[k]
            ends[k] = total
            return total

        lax.fori_loop(0, docs, end, jnp.int32(0))

        def clear(k, carry):
            acc[k] = jnp.zeros(acc.shape[1:], jnp.float32)
            return carry

        lax.fori_loop(0, docs, clear, 0)

    block = g_ref[0]
    widened = block.astype(jnp.float32)
    squares = jnp.sum(widened * widened, axis=0, keepdims=True)
    weight = 1.0 / (squares / (draws - 1) + epsilon)
    weights[...] = jnp.transpose(jnp.broadcast_to(weight, (128, half)))
    turned[...] = jnp.transpose(block)

    base = (step // 2) * tokens + rank[0] * piece + lax.rem(step, 2) * half

    first_doc = lax.while_loop(lambda k: ends[k] <= base, lambda k: k + 1, jnp.int32(0))

    def body(state):
        at, doc = state
        row = pl.multiple_of(at // tile * tile, tile)
        stop = jnp.minimum(row + tile, ends[doc] - base)
        places = row + lax.broadcasted_iota(jnp.int32, (tile, 128), 0)
        inside = (places >= at) & (places < stop)
        wt = jnp.where(inside, weights[pl.ds(row, tile), :], 0.0)
        wt = jnp.concatenate([wt] * (strip // 128), axis=1)
        lhs = turned[pl.ds(row, tile), :]
        for n in range(queries // strip):
            cov = jnp.dot(
                lhs, paired[:, n * strip:(n + 1) * strip], preferred_element_type=jnp.float32
            )
            signed = cov * jnp.abs(cov) * wt
            part = jnp.sum(signed.reshape(tile // 8, 8, strip), axis=0)
            acc[doc, :, n * strip:(n + 1) * strip] += part
        return stop, jnp.where(stop >= ends[doc] - base, doc + 1, doc)

    lax.while_loop(lambda state: state[0] < half, body, (jnp.int32(0), first_doc))

    @pl.when(step == pl.num_programs(0) - 1)
    def _():
        chosen = paired[...].astype(jnp.float32)
        squares = jnp.sum(chosen * chosen, axis=0, keepdims=True)
        scale = 1.0 / (squares / (draws - 1) + epsilon) / ((draws - 1) * (draws - 1))

        def finish(k, carry):
            pooled = jnp.sum(acc[k], axis=0, keepdims=True)
            out_ref[pl.ds(k, 1), :] = pooled * scale / lengths[k].astype(jnp.float32)
            return carry

        lax.fori_loop(0, docs, finish, 0)


def pool(lengths, slots, rank, pieces, query, tokens, piece):
    chunks, draws, half = pieces.shape
    queries = query.shape[1]
    docs = lengths.shape[0]
    return pl.pallas_call(
        functools.partial(pool_kernel, tokens=tokens, piece=piece),
        out_shape=jax.ShapeDtypeStruct((docs, queries), jnp.float32),
        grid_spec=pltpu.PrefetchScalarGridSpec(
            num_scalar_prefetch=3,
            grid=(chunks,),
            in_specs=[
                pl.BlockSpec((1, draws, half), lambda i, *_: (i, 0, 0)),
                pl.BlockSpec((draws, queries), lambda i, *_: (0, 0)),
            ],
            out_specs=pl.BlockSpec((docs, queries), lambda i, *_: (0, 0)),
            scratch_shapes=[
                pltpu.VMEM((draws, queries), jnp.float32),
                pltpu.VMEM((draws, queries), jnp.bfloat16),
                pltpu.VMEM((docs, 8, queries), jnp.float32),
                pltpu.VMEM((half, draws), jnp.bfloat16),
                pltpu.VMEM((half, 128), jnp.float32),
                pltpu.SMEM((docs,), jnp.int32),
            ],
        ),
        compiler_params=pltpu.CompilerParams(
            dimension_semantics=("arbitrary",), vmem_limit_bytes=48 << 20
        ),
    )(lengths, slots, rank, pieces, query)


def scatter_kernel(n_t, p_ref, out_ref, near, total, far, s1, r1, s2, r2):
    t = lax.axis_index("train")
    q = lax.axis_index("query")
    n_m = n_t // 2
    m, c = t // 2, lax.rem(t, 2)
    sibling = 2 * m + 1 - c
    barrier = pltpu.get_barrier_semaphore()
    pl.semaphore_signal(barrier, inc=1, device_id=(sibling, q), device_id_type=MESH)
    for k in range(1, n_m):
        other = 2 * lax.rem(m + k, n_m) + c
        pl.semaphore_signal(barrier, inc=1, device_id=(other, q), device_id_type=MESH)
    pl.semaphore_wait(barrier, n_m)
    started = []
    chips = [lax.rem(m + k, n_m) for k in range(1, n_m)] + [m]
    for chip in chips:
        copy = remote(p_ref.at[chip, 1 - c], near.at[chip], s1.at[chip], r1.at[chip], (sibling, q))
        copy.start()
        started.append(copy)
    for chip in chips:
        remote(near.at[chip], near.at[chip], s1.at[chip], r1.at[chip], (sibling, q)).wait_recv()
        total[chip] = p_ref[chip, c] + near[chip]
        if chip is not m:
            copy = remote(total.at[chip], far.at[m], s2.at[chip], r2.at[m], (2 * chip + c, q))
            copy.start()
            started.append(copy)
    result = total[m]
    for k in range(1, n_m):
        chip = lax.rem(m + n_m - k, n_m)
        remote(far.at[chip], far.at[chip], s2.at[chip], r2.at[chip], (2 * chip + c, q)).wait_recv()
        result = result + far[chip]
    out_ref[...] = result
    for copy in started:
        copy.wait_send()


def scatter(partial, n_t):
    docs, queries = partial.shape
    here = docs // n_t
    n_m = n_t // 2
    dma = pltpu.SemaphoreType.DMA
    block = pltpu.VMEM((n_m, here, queries), jnp.float32)
    return pl.pallas_call(
        functools.partial(scatter_kernel, n_t),
        out_shape=jax.ShapeDtypeStruct((here, queries), jnp.float32),
        in_specs=[pl.BlockSpec(memory_space=pltpu.VMEM)],
        out_specs=pl.BlockSpec(memory_space=pltpu.VMEM),
        scratch_shapes=[block, block, block, dma((n_m,)), dma((n_m,)), dma((n_m,)), dma((n_m,))],
        compiler_params=pltpu.CompilerParams(
            collective_id=1, has_side_effects=True, vmem_limit_bytes=16 << 20
        ),
    )(partial.reshape(n_m, 2, here, queries))


def shards(train_losses, query_losses, chain_slots, doc_lengths):
    n_t = lax.axis_size("train")
    n_q = lax.axis_size("query")
    draws_here, tokens = train_losses.shape
    queries = query_losses.shape[1]
    draws = draws_here * n_t
    piece = tokens // n_t
    pieces, query = gather(train_losses, query_losses, n_t, n_q)
    rank = lax.axis_index("train").astype(jnp.int32).reshape(1)
    partial = pool(
        doc_lengths, chain_slots, rank,
        pieces.reshape(n_q * 2, draws, piece // 2), query.reshape(draws, queries), tokens, piece,
    )
    return scatter(partial, n_t)


def solution(mesh):
    in_specs = (P("train", "query"), P("train", "query"), P(), P())
    out_specs = P("train", "query")
    return jax.shard_map(shards, mesh=mesh, in_specs=in_specs, out_specs=out_specs, check_vma=False)
```

time: 253 us -> 103 us (0.41)
  waiting for transfers between devices: 144 us -> 0 us
  Pallas kernels: 0 us -> 98.7 us
  matrix products: 57.6 us -> 0 us
  other arithmetic: 16.6 us -> 0 us
  between operations: 13.3 us -> 0.04 us
  local copies, waits for them, and re-layouts: 14.3 us -> 4.48 us
  starting transfers between devices: 6.48 us -> 0 us
    pallas_call x0 -> x3, Pallas kernels: none -> 98.7 us  [the longest x1 51.8 us: gather(): pl.pallas_call(functools.partial(gather_kernel, n_t, n_q), out_shape=(jax...]
    all_to_all x1 -> x0, waiting for transfers between devices: 65.1 us -> none  [shards(): lax.all_to_all(deal_columns(train_losses, train_parts), 'train', split_ax...]
    dot_general x16 -> x0, matrix products: 57.6 us -> none  [the longest x8 38.9 us: add_piece(): lax.dot_general(member, signed, (((0,), (0,)), ((), ())), precision=highe...]
    all_gather x2 -> x0, waiting for transfers between devices: 46.4 us -> none  [the longest x1 46.3 us: shards(): portion = lax.all_gather(centered_here, 'query', axis=1, tiled=True)]
    reduce_scatter x1 -> x0, waiting for transfers between devices: 31.5 us -> none  [shards(): lax.psum_scatter(running, 'train', scatter_dimension=0, tiled=True)]
    reduce_sum x11 -> x0, other arithmetic: 11.6 us -> none  [the longest x9 9.73 us: row_scale(): jnp.sum(widened * widened, axis=0) / (centered.shape[0] - 1) + epsilon]
    all_to_all x1 -> x0, starting transfers between devices: 6.35 us -> none  [shards(): lax.all_to_all(deal_columns(train_losses, train_parts), 'train', split_ax...]
    transpose x1 -> x0, local copies, waits for them, and re-layouts: 6.3 us -> none  [deal_columns(): block.reshape(height, width // groups, groups).transpose(0, 2, 1)]
  transfers between devices with their start and end apart: 4 -> 0, of which waited for: 3 -> 0; matrix products, arithmetic and copies ran while one was open for 3% -> 0% of each run, Pallas kernels for 0% -> 0%
where the time goes in v1:
time: 103 us
  Pallas kernels  98.7 us (96%)
  local copies, waits for them, and re-layouts  4.48 us (4%)
    pallas_call x1, Pallas kernels, gather(): pl.pallas_call(functools.partial(gather_kernel, n_t, n_q), out_shape=(jax...  51.8 us
    pallas_call x1, Pallas kernels, pool(): pl.pallas_call(functools.partial(pool_kernel, tokens=tokens, piece=piece)...  24.2 us
    pallas_call x1, Pallas kernels, scatter(): pl.pallas_call(functools.partial(scatter_kernel, n_t), out_shape=jax.Shap...  22.7 us
    unnamed x9, local copies, waits for them, and re-layouts  4.48 us

profile of v1, /device:TPU:0, one launch (start us, length us, event | category | flops | bytes accessed | tf_op | source)
XLA Modules:
  0.0 103.2 jit_solution(6002736293417482556)
XLA Ops:
  0.0 0.0 copy-start
  0.0 1.6 %copy-done = f32[32,16384]{1,0:T(8,128)S(1)} copy-done((f32[32,16384]{1,0:T(8,128)S(1)}, f32[32,16384]{1,0:T(8,128)}, u32[]{:S(2)}) %copy-start) | copy-done | bytes 2097176
  1.6 0.0 copy-start.1
  1.6 0.9 copy-done.1
  2.5 51.8 %shard_map.46 = (bf16[4,2,8,32,1024]{4,3,2,1,0:T(8,128)(2,1)S(1)}, bf16[8,32,2048]{2,1,0:T(8,128)(2,1)S(1)}) custom-call(f32[32,16384]{1,0:T(8,128)S(1)} %copy-done, f32[32,2048]{1,0:T(8,128)S(1)} %copy-done.1), custom_call_target="tpu_custom_call" | custom-call | tf_op jit(solution)/shard_map/pallas_call | solution.py:174
  54.3 0.0 copy-start.2
  54.3 0.6 copy-done.2
  55.0 0.0 copy-start.3
  55.0 0.7 copy-done.3
  55.6 24.2 %shard_map.47 = f32[64,2048]{1,0:T(8,128)S(1)} custom-call(s32[64]{0:T(128)S(1)} %copy-done.2, s32[32]{0:T(128)S(1)} %copy-done.3, s32[1]{0:T(128)} %bitcast.rank, bf16[8,256,1024]{2,1,0:T(8,128)(2,1)S(1)} %bitcast.4, bf16[256,2048]{1,0:T(8,128)(2,1)S(1)} %bitcast.6), custom_call_target="tpu_custom_call" | custom-call | tf_op jit(solution)/shard_map/pallas_call | solution.py:288
  79.8 22.7 %shard_map.48 = f32[8,2048]{1,0:T(8,128)S(1)} custom-call(f32[4,2,8,2048]{3,2,1,0:T(8,128)S(1)} %bitcast.5), custom_call_target="tpu_custom_call" | custom-call | tf_op jit(solution)/shard_map/pallas_call | solution.py:355
  102.6 0.6 copy.6
Async XLA Ops:
  0.0 1.6 %copy-start = (f32[32,16384]{1,0:T(8,128)S(1)}, f32[32,16384]{1,0:T(8,128)}, u32[]{:S(2)}) copy-start(f32[32,16384]{1,0:T(8,128)} %x_ref.1) | copy-start | bytes 6291460
  1.6 0.9 copy-start.1
  54.3 0.7 copy-start.2
  55.0 0.7 copy-start.3

commit v2 on v1

v2 whole, which is shorter than its diff:
```python
import functools

import jax
import jax.numpy as jnp
from jax import lax
from jax.experimental import pallas as pl
from jax.experimental.pallas import tpu as pltpu
from jax.sharding import PartitionSpec as P

MESH = pl.DeviceIdType.MESH
epsilon = 1e-06
per_chain = 8


def remote(src, dst, send, recv, device):
    return pltpu.make_async_remote_copy(
        src_ref=src, dst_ref=dst, send_sem=send, recv_sem=recv, device_id=device, device_id_type=MESH
    )


chunks = 4


def fused_kernel(
    n_t, n_q, x_ref, y_ref, slots_ref, lengths_ref, out_ref,
    sums, parts, means, cent, centq, held, whole_q, turned, scales, acc,
    s1, r1, s2, r2, sa, ra, sq, rq, sf, rf, sb, rb, sr, rr, s0, r0, sh, rh, local_sem,
):
    t = lax.axis_index("train")
    q = lax.axis_index("query")
    n_m, n_a = n_t // 2, n_q // 2
    m, c = t // 2, lax.rem(t, 2)
    sibling = 2 * m + 1 - c
    a, b = q // 2, lax.rem(q, 2)
    partner = 2 * a + 1 - b
    others = [lax.rem(a + k, n_a) for k in range(1, n_a)]
    columns = [2 * other + b for other in others]
    diagonals = [2 * other + 1 - b for other in others]
    size = cent.shape[3]
    half = size // 2
    piece = chunks * size
    queries = y_ref.shape[1]
    spread = queries // n_t
    draws = x_ref.shape[0] * n_t
    tokens = x_ref.shape[1]
    docs = out_ref.shape[0]

    barrier = pltpu.get_barrier_semaphore()
    for k in range(1, n_t):
        pl.semaphore_signal(barrier, inc=1, device_id=(lax.rem(t + k, n_t), q), device_id_type=MESH)
    for target in [partner] + columns:
        pl.semaphore_signal(barrier, inc=1, device_id=(t, target), device_id_type=MESH)
    for r in range(n_t):
        sums[r, :, 0:piece] = jnp.sum(x_ref[:, r * piece:(r + 1) * piece], axis=0, keepdims=True)
        sums[r, :, piece:piece + spread] = jnp.sum(
            y_ref[:, r * spread:(r + 1) * spread], axis=0, keepdims=True
        )
    pl.semaphore_wait(barrier, n_t - 1 + n_a)

    sends, sources = [sibling], [sibling]
    for k in range(1, n_m):
        up, down = lax.rem(m + k, n_m), lax.rem(m + n_m - k, n_m)
        sends += [2 * up + c, 2 * up + 1 - c]
        sources += [2 * down + c, 2 * down + 1 - c]

    started = []
    for r in sends:
        copy = remote(sums.at[r], parts.at[t], s1.at[r], r1.at[t], (r, q))
        copy.start()
        started.append(copy)
    total = sums[t]
    for r in sources:
        remote(parts.at[r], parts.at[r], s1.at[r], r1.at[r], (r, q)).wait_recv()
        total = total + parts[r]
    means[t] = total / draws
    for r in sends:
        copy = remote(means.at[t], means.at[t], s2.at[r], r2.at[t], (r, q))
        copy.start()
        started.append(copy)

    def center(r, j):
        begin = pl.multiple_of(r * piece + j * size, 128)
        mean = means[r, :, j * size:(j + 1) * size]
        cent[r, j] = (x_ref[:, pl.ds(begin, size)] - mean).astype(jnp.bfloat16)

    def center_query(r):
        begin = pl.multiple_of(r * spread, 128)
        centq[:, pl.ds(begin, spread)] = (
            y_ref[:, pl.ds(begin, spread)] - means[r, :, piece:piece + spread]
        ).astype(jnp.bfloat16)

    def spread_block(src, j, tp):
        remote(src, held.at[q, j, tp], sb.at[j], rb.at[j, tp], (t, partner)).start()
        for k in range(n_a - 1):
            remote(
                src, held.at[q, j, tp], sr.at[j, others[k]], rr.at[j, tp, a], (t, columns[k])
            ).start()

    def pass_on(j, tp):
        block = held.at[partner, j, tp]
        remote(block, block, sb.at[j], rb.at[j, tp], (t, partner)).wait_recv()
        first = held.at[partner, j, tp, :, pl.ds(0, half)]
        for k in range(n_a - 1):
            remote(first, first, s0.at[j, others[k]], r0.at[j, a], (t, columns[k])).start()
        for k in range(n_a - 1):
            block = held.at[columns[k], j, tp]
            remote(
                block, block, sr.at[j, others[k]], rr.at[j, tp, others[k]], (t, columns[k])
            ).wait_recv()
            second = held.at[columns[k], j, tp, :, pl.ds(half, half)]
            remote(second, second, sh.at[j, others[k]], rh.at[j, others[k]], (t, partner)).start()

    locals_ = []
    for j in range(chunks):
        center(t, j)
        copy = pltpu.make_async_copy(cent.at[t, j], held.at[q, j, t], local_sem.at[j])
        copy.start()
        locals_.append(copy)
    center_query(t)
    for j in range(chunks):
        for r in sends:
            if j == 0:
                remote(means.at[r], means.at[r], s2.at[r], r2.at[r], (r, q)).wait_recv()
            center(r, j)
            remote(cent.at[r, j], held.at[q, j, t], sa.at[j], ra.at[j, t], (r, q)).start()
        if j == 0:
            spread_block(cent.at[t, 0], 0, t)
            for r in sends:
                center_query(r)
            for k in range(1, n_m):
                up = lax.rem(m + k, n_m)
                copy = remote(centq, whole_q.at[t], sq.at[up], rq.at[m], (2 * up + c, q))
                copy.start()
                started.append(copy)
            copy = remote(centq, whole_q.at[t], sf.at[m], rf.at[m], (sibling, q))
            copy.start()
            started.append(copy)
            ownq = pltpu.make_async_copy(centq, whole_q.at[t], local_sem.at[chunks])
            ownq.start()
            locals_.append(ownq)

    def stage(j, units, first=False):
        if not first:
            spread_block(cent.at[t, j], j, t)
        before = t
        due = 0
        for i, tp in enumerate(sources):
            block = held.at[q, j, tp]
            remote(block, block, sa.at[j], ra.at[j, tp], (tp, q)).wait_recv()
            spread_block(block, j, tp)
            pass_on(j, before)
            before = tp
            while due < len(units) and due * (n_t - 1) <= i * len(units):
                units[due]()
                due += 1
        pass_on(j, before)
        for unit in units[due:]:
            unit()

    def settle(j):
        for k in range(n_a - 1):
            first = held.at[diagonals[k], j, :, :, pl.ds(0, half)]
            remote(first, first, s0.at[j, others[k]], r0.at[j, others[k]], (t, columns[k])).wait_recv()
            second = held.at[diagonals[k], j, :, :, pl.ds(half, half)]
            remote(second, second, sh.at[j, others[k]], rh.at[j, others[k]], (t, partner)).wait_recv()

    wide = jnp.broadcast_to(lengths_ref[...].astype(jnp.float32), (docs, docs))
    row = lax.broadcasted_iota(jnp.int32, (docs, docs), 0)
    column = lax.broadcasted_iota(jnp.int32, (docs, docs), 1)
    doc_ends = jnp.sum(jnp.where(column <= row, wide, 0.0), axis=1, keepdims=True)
    doc_starts = jnp.sum(jnp.where(column < row, wide, 0.0), axis=1, keepdims=True)
    strip = min(256, queries)

    def unit(col, j):
        block = held[col, j].reshape(draws, size)
        widened = block.astype(jnp.float32)
        squares = jnp.sum(widened * widened, axis=0, keepdims=True)
        weight = 1.0 / (squares / (draws - 1) + epsilon)
        high = weight.astype(jnp.bfloat16).astype(jnp.float32)
        low = weight - high
        base = col * tokens + t * piece + j * size
        places = (base + lax.broadcasted_iota(jnp.int32, (docs, size), 1)).astype(jnp.float32)
        inside = (places >= doc_starts) & (places < doc_ends)
        member = jnp.concatenate(
            [jnp.where(inside, high, 0.0), jnp.where(inside, low, 0.0)], axis=0
        ).astype(jnp.bfloat16)

        def add_strip(n, carry):
            begin = pl.multiple_of(n * strip, strip)
            cov = jnp.dot(
                turned[pl.ds(begin, strip), :], block, preferred_element_type=jnp.float32
            )
            signed = cov * jnp.abs(cov)
            top = signed.astype(jnp.bfloat16)
            rest = (signed - top.astype(jnp.float32)).astype(jnp.bfloat16)
            dims = (((1,), (1,)), ((), ()))
            pooled = lax.dot_general(top, member, dims, preferred_element_type=jnp.float32)
            pooled += lax.dot_general(rest, member, dims, preferred_element_type=jnp.float32)
            acc[pl.ds(begin, strip), :] += pooled
            return carry

        lax.fori_loop(0, queries // strip, add_strip, 0)

    order = [q, partner] + columns + diagonals

    acc[...] = jnp.zeros_like(acc)
    stage(0, [], first=True)
    for k in range(1, n_m):
        down = lax.rem(m + n_m - k, n_m)
        block = whole_q.at[2 * down + c]
        remote(block, block, sq.at[down], rq.at[down], (2 * down + c, q)).wait_recv()
        copy = remote(block, block, sf.at[down], rf.at[down], (sibling, q))
        copy.start()
        started.append(copy)
    for k in range(n_m):
        block = whole_q.at[2 * k + 1 - c]
        remote(block, block, sf.at[k], rf.at[k], (sibling, q)).wait_recv()
    for copy in locals_:
        copy.wait()

    slots = jnp.broadcast_to(slots_ref[...].astype(jnp.float32), (draws, draws // per_chain))
    row = lax.broadcasted_iota(jnp.int32, slots.shape, 0)
    slot = lax.broadcasted_iota(jnp.int32, slots.shape, 1)
    offset = row - slot * per_chain
    chosen = jnp.where(
        (offset >= 0) & (offset < per_chain), slots * per_chain + offset.astype(jnp.float32), 0.0
    )
    source = jnp.sum(chosen, axis=1, keepdims=True)
    place = lax.broadcasted_iota(jnp.int32, (draws, draws), 1).astype(jnp.float32)
    moves = jnp.where(place == source, 1.0, 0.0).astype(jnp.bfloat16)
    everything = whole_q[...].reshape(draws, queries)
    for n in range(queries // strip):
        part = jnp.dot(
            moves, everything[:, n * strip:(n + 1) * strip], preferred_element_type=jnp.float32
        )
        squares = jnp.sum(part * part, axis=0, keepdims=True)
        scales[:, n * strip:(n + 1) * strip] = (
            1.0 / (squares / (draws - 1) + epsilon) / ((draws - 1) * (draws - 1))
        )
        turned[n * strip:(n + 1) * strip, :] = jnp.transpose(part).astype(jnp.bfloat16)

    def step(j, carry):
        units = [functools.partial(unit, col, j - 1) for col in order]
        units[n_a + 1] = lambda: (settle(j - 1), unit(order[n_a + 1], j - 1))
        stage(j, units)
        return carry

    lax.fori_loop(1, chunks, step, 0)

    def last(i, carry):
        col = jnp.int32(0)
        for k in range(n_q):
            col = jnp.where(i == k, order[k], col)
        unit(col, chunks - 1)
        return carry

    lax.fori_loop(0, n_a + 1, last, 0)
    settle(chunks - 1)
    lax.fori_loop(n_a + 1, n_q, last, 0)

    for n in range(queries // strip):
        flat = jnp.transpose(acc[n * strip:(n + 1) * strip, :])
        out_ref[:, n * strip:(n + 1) * strip] = (
            (flat[0:docs] + flat[docs:2 * docs])
            * scales[:, n * strip:(n + 1) * strip]
            / (doc_ends - doc_starts)
        )

    for copy in started:
        copy.wait_send()
    for j in range(chunks):
        sent = cent.at[pl.ds(0, n_t - 1), j]
        remote(sent, sent, sa.at[j], ra.at[j, 0], (sibling, q)).wait_send()
        full = held.at[q, j]
        remote(full, full, sb.at[j], rb.at[j, 0], (t, partner)).wait_send()
        for k in range(n_a - 1):
            remote(full, full, sr.at[j, others[k]], rr.at[j, 0, 0], (t, partner)).wait_send()
            first = held.at[q, j, :, :, pl.ds(0, half)]
            remote(first, first, s0.at[j, others[k]], r0.at[j, 0], (t, partner)).wait_send()
            remote(first, first, sh.at[j, others[k]], rh.at[j, 0], (t, partner)).wait_send()


def fused(train_losses, query_losses, chain_slots, doc_lengths, n_t, n_q):
    draws_here, tokens = train_losses.shape
    queries = query_losses.shape[1]
    docs = doc_lengths.shape[0]
    draws = draws_here * n_t
    size = tokens // n_t // chunks
    width = chunks * size + queries // n_t
    n_m, n_a = n_t // 2, n_q // 2
    dma = pltpu.SemaphoreType.DMA
    bf16 = jnp.bfloat16
    vmem = pl.BlockSpec(memory_space=pltpu.VMEM)
    return pl.pallas_call(
        functools.partial(fused_kernel, n_t, n_q),
        out_shape=jax.ShapeDtypeStruct((docs, queries), jnp.float32),
        in_specs=[vmem] * 4,
        out_specs=vmem,
        scratch_shapes=[
            pltpu.VMEM((n_t, 1, width), jnp.float32),
            pltpu.VMEM((n_t, 1, width), jnp.float32),
            pltpu.VMEM((n_t, 1, width), jnp.float32),
            pltpu.VMEM((n_t, chunks, draws_here, size), bf16),
            pltpu.VMEM((draws_here, queries), bf16),
            pltpu.VMEM((n_q, chunks, n_t, draws_here, size), bf16),
            pltpu.VMEM((n_t, draws_here, queries), bf16),
            pltpu.VMEM((queries, draws), bf16),
            pltpu.VMEM((1, queries), jnp.float32),
            pltpu.VMEM((queries, 2 * docs), jnp.float32),
            dma((n_t,)), dma((n_t,)), dma((n_t,)), dma((n_t,)),
            dma((chunks,)), dma((chunks, n_t)),
            dma((n_m,)), dma((n_m,)), dma((n_m,)), dma((n_m,)),
            dma((chunks,)), dma((chunks, n_t)),
            dma((chunks, n_a)), dma((chunks, n_t, n_a)),
            dma((chunks, n_a)), dma((chunks, n_a)),
            dma((chunks, n_a)), dma((chunks, n_a)),
            dma((chunks + 1,)),
        ],
        compiler_params=pltpu.CompilerParams(
            collective_id=0, has_side_effects=True, vmem_limit_bytes=48 << 20
        ),
    )(train_losses, query_losses, chain_slots.reshape(1, -1), doc_lengths.reshape(1, -1))


def scatter_kernel(n_t, p_ref, out_ref, near, total, far, s1, r1, s2, r2):
    t = lax.axis_index("train")
    q = lax.axis_index("query")
    n_m = n_t // 2
    m, c = t // 2, lax.rem(t, 2)
    sibling = 2 * m + 1 - c
    barrier = pltpu.get_barrier_semaphore()
    pl.semaphore_signal(barrier, inc=1, device_id=(sibling, q), device_id_type=MESH)
    for k in range(1, n_m):
        other = 2 * lax.rem(m + k, n_m) + c
        pl.semaphore_signal(barrier, inc=1, device_id=(other, q), device_id_type=MESH)
    pl.semaphore_wait(barrier, n_m)
    started = []
    chips = [lax.rem(m + k, n_m) for k in range(1, n_m)] + [m]
    for chip in chips:
        copy = remote(p_ref.at[chip, 1 - c], near.at[chip], s1.at[chip], r1.at[chip], (sibling, q))
        copy.start()
        started.append(copy)
    for chip in chips:
        remote(near.at[chip], near.at[chip], s1.at[chip], r1.at[chip], (sibling, q)).wait_recv()
        total[chip] = p_ref[chip, c] + near[chip]
        if chip is not m:
            copy = remote(total.at[chip], far.at[m], s2.at[chip], r2.at[m], (2 * chip + c, q))
            copy.start()
            started.append(copy)
    result = total[m]
    for k in range(1, n_m):
        chip = lax.rem(m + n_m - k, n_m)
        remote(far.at[chip], far.at[chip], s2.at[chip], r2.at[chip], (2 * chip + c, q)).wait_recv()
        result = result + far[chip]
    out_ref[...] = result
    for copy in started:
        copy.wait_send()


def scatter(partial, n_t):
    docs, queries = partial.shape
    here = docs // n_t
    n_m = n_t // 2
    dma = pltpu.SemaphoreType.DMA
    block = pltpu.VMEM((n_m, here, queries), jnp.float32)
    return pl.pallas_call(
        functools.partial(scatter_kernel, n_t),
        out_shape=jax.ShapeDtypeStruct((here, queries), jnp.float32),
        in_specs=[pl.BlockSpec(memory_space=pltpu.VMEM)],
        out_specs=pl.BlockSpec(memory_space=pltpu.VMEM),
        scratch_shapes=[block, block, block, dma((n_m,)), dma((n_m,)), dma((n_m,)), dma((n_m,))],
        compiler_params=pltpu.CompilerParams(
            collective_id=1, has_side_effects=True, vmem_limit_bytes=16 << 20
        ),
    )(partial.reshape(n_m, 2, here, queries))


def shards(train_losses, query_losses, chain_slots, doc_lengths):
    n_t = lax.axis_size("train")
    n_q = lax.axis_size("query")
    partial = fused(train_losses, query_losses, chain_slots, doc_lengths, n_t, n_q)
    return scatter(partial, n_t)


def solution(mesh):
    in_specs = (P("train", "query"), P("train", "query"), P(), P())
    out_specs = P("train", "query")
    return jax.shard_map(shards, mesh=mesh, in_specs=in_specs, out_specs=out_specs, check_vma=False)
```

time: 103 us -> 154 us (1.50)
  Pallas kernels: 98.7 us -> 148 us
    pallas_call x2 -> x1, Pallas kernels: 76 us -> 134 us  [fused(): pl.pallas_call(functools.partial(fused_kernel, n_t, n_q), out_shape=jax.S...]
    pallas_call x1, Pallas kernels: 22.7 us -> 14.5 us  [scatter(): pl.pallas_call(functools.partial(scatter_kernel, n_t), out_shape=jax.Shap...]
where the time goes in v2:
time: 154 us; the launch traced here: 153 us
  Pallas kernels  148 us (96%)
  local copies, waits for them, and re-layouts  4.48 us (3%)
    pallas_call x1, Pallas kernels, fused(): pl.pallas_call(functools.partial(fused_kernel, n_t, n_q), out_shape=jax.S...  134 us
    pallas_call x1, Pallas kernels, scatter(): pl.pallas_call(functools.partial(scatter_kernel, n_t), out_shape=jax.Shap...  14.5 us
    unnamed x9, local copies, waits for them, and re-layouts  4.48 us

profile of v2, /device:TPU:0, one launch (start us, length us, event | category | flops | bytes accessed | tf_op | source)
XLA Modules:
  0.0 152.7 jit_solution(14453771994795817978)
XLA Ops:
  0.0 0.0 copy-start
  0.0 1.6 %copy-done = f32[32,16384]{1,0:T(8,128)S(1)} copy-done((f32[32,16384]{1,0:T(8,128)S(1)}, f32[32,16384]{1,0:T(8,128)}, u32[]{:S(2)}) %copy-start) | copy-done | bytes 2097176
  1.6 0.0 copy-start.1
  1.6 0.9 copy-done.1
  2.5 0.0 copy-start.2
  2.5 0.7 copy-done.2
  3.2 0.0 copy-start.3
  3.2 0.7 copy-done.3
  3.9 133.8 %shard_map.46 = f32[64,2048]{1,0:T(8,128)S(1)} custom-call(f32[32,16384]{1,0:T(8,128)S(1)} %copy-done, f32[32,2048]{1,0:T(8,128)S(1)} %copy-done.1, s32[1,32]{1,0:T(1,128)S(1)} %bitcast.4, s32[1,64]{1,0:T(1,128)S(1)} %bitcast.5), custom_call_target="tpu_custom_call" | custom-call | tf_op jit(solution)/shard_map/pallas_call | solution.py:294
  137.6 14.5 %shard_map.47 = f32[8,2048]{1,0:T(8,128)S(1)} custom-call(f32[4,2,8,2048]{3,2,1,0:T(8,128)S(1)} %bitcast.3), custom_call_target="tpu_custom_call" | custom-call | tf_op jit(solution)/shard_map/pallas_call | solution.py:366
  152.1 0.6 copy.6
Async XLA Ops:
  0.0 1.6 %copy-start = (f32[32,16384]{1,0:T(8,128)S(1)}, f32[32,16384]{1,0:T(8,128)}, u32[]{:S(2)}) copy-start(f32[32,16384]{1,0:T(8,128)} %x_ref.1) | copy-start | bytes 6291460
  1.6 0.9 copy-start.1
  2.5 0.7 copy-start.2
  3.2 0.7 copy-start.3

commit v3 on v2

--- a/solution.py
+++ b/solution.py
@@ -18,7 +18,8 @@
     )
 
 
-chunks = 4
+chunks = 2
+delay = 4
 
 
 def fused_kernel(
@@ -139,21 +140,26 @@
             ownq.start()
             locals_.append(ownq)
 
+    ranks = [t] + sources
+    lag = min(delay, n_t - 1)
+
     def stage(j, units, first=False):
-        if not first:
-            spread_block(cent.at[t, j], j, t)
-        before = t
         due = 0
-        for i, tp in enumerate(sources):
-            block = held.at[q, j, tp]
-            remote(block, block, sa.at[j], ra.at[j, tp], (tp, q)).wait_recv()
-            spread_block(block, j, tp)
-            pass_on(j, before)
-            before = tp
-            while due < len(units) and due * (n_t - 1) <= i * len(units):
+        for i, tp in enumerate(ranks):
+            if i == 0:
+                if not first:
+                    spread_block(cent.at[t, j], j, t)
+            else:
+                block = held.at[q, j, tp]
+                remote(block, block, sa.at[j], ra.at[j, tp], (tp, q)).wait_recv()
+                spread_block(block, j, tp)
+            if i >= lag:
+                pass_on(j, ranks[i - lag])
+            elif not first:
+                pass_on(j - 1, ranks[n_t - lag + i])
+            while due < len(units) and lag + due * (n_t - lag) // len(units) <= i + 1:
                 units[due]()
                 due += 1
-        pass_on(j, before)
         for unit in units[due:]:
             unit()
 
@@ -169,7 +175,7 @@
     column = lax.broadcasted_iota(jnp.int32, (docs, docs), 1)
     doc_ends = jnp.sum(jnp.where(column <= row, wide, 0.0), axis=1, keepdims=True)
     doc_starts = jnp.sum(jnp.where(column < row, wide, 0.0), axis=1, keepdims=True)
-    strip = min(256, queries)
+    strip = min(512, queries)
 
     def unit(col, j):
         block = held[col, j].reshape(draws, size)
@@ -199,7 +205,7 @@
             acc[pl.ds(begin, strip), :] += pooled
             return carry
 
-        lax.fori_loop(0, queries // strip, add_strip, 0)
+        lax.fori_loop(0, queries // strip, add_strip, 0, unroll=True)
 
     order = [q, partner] + columns + diagonals
 
@@ -246,6 +252,8 @@
         return carry
 
     lax.fori_loop(1, chunks, step, 0)
+    for i in range(lag):
+        pass_on(chunks - 1, ranks[n_t - lag + i])
 
     def last(i, carry):
         col = jnp.int32(0)

time: 154 us -> 93 us (0.60)
  Pallas kernels: 148 us -> 88.3 us
    pallas_call x1, Pallas kernels: 134 us -> 76.7 us  [fused(): pl.pallas_call(functools.partial(fused_kernel, n_t, n_q), out_shape=jax.S...]
    pallas_call x1, Pallas kernels: 14.5 us -> 11.6 us  [scatter(): pl.pallas_call(functools.partial(scatter_kernel, n_t), out_shape=jax.Shap...]
where the time goes in v3:
time: 93 us; the launch traced here: 92.8 us
  Pallas kernels  88.3 us (95%)
  local copies, waits for them, and re-layouts  4.48 us (5%)
    pallas_call x1, Pallas kernels, fused(): pl.pallas_call(functools.partial(fused_kernel, n_t, n_q), out_shape=jax.S...  76.7 us
    pallas_call x1, Pallas kernels, scatter(): pl.pallas_call(functools.partial(scatter_kernel, n_t), out_shape=jax.Shap...  11.6 us
    unnamed x9, local copies, waits for them, and re-layouts  4.48 us

profile of v3, /device:TPU:0, one launch (start us, length us, event | category | flops | bytes accessed | tf_op | source)
XLA Modules:
  0.0 92.8 jit_solution(2012794422725056608)
XLA Ops:
  0.0 0.0 copy-start
  0.0 1.6 %copy-done = f32[32,16384]{1,0:T(8,128)S(1)} copy-done((f32[32,16384]{1,0:T(8,128)S(1)}, f32[32,16384]{1,0:T(8,128)}, u32[]{:S(2)}) %copy-start) | copy-done | bytes 2097176
  1.6 0.0 copy-start.1
  1.6 0.9 %copy-done.1 = f32[32,2048]{1,0:T(8,128)S(1)} copy-done((f32[32,2048]{1,0:T(8,128)S(1)}, f32[32,2048]{1,0:T(8,128)}, u32[]{:S(2)}) %copy-start.1) | copy-done | bytes 262168
  2.5 0.0 copy-start.2
  2.5 0.7 copy-done.2
  3.2 0.0 copy-start.3
  3.2 0.7 copy-done.3
  3.9 76.7 %shard_map.46 = f32[64,2048]{1,0:T(8,128)S(1)} custom-call(f32[32,16384]{1,0:T(8,128)S(1)} %copy-done, f32[32,2048]{1,0:T(8,128)S(1)} %copy-done.1, s32[1,32]{1,0:T(1,128)S(1)} %bitcast.4, s32[1,64]{1,0:T(1,128)S(1)} %bitcast.5), custom_call_target="tpu_custom_call" | custom-call | tf_op jit(solution)/shard_map/pallas_call | solution.py:302
  80.6 11.6 %shard_map.47 = f32[8,2048]{1,0:T(8,128)S(1)} custom-call(f32[4,2,8,2048]{3,2,1,0:T(8,128)S(1)} %bitcast.3), custom_call_target="tpu_custom_call" | custom-call | tf_op jit(solution)/shard_map/pallas_call | solution.py:374
  92.2 0.6 copy.6
Async XLA Ops:
  0.0 1.6 %copy-start = (f32[32,16384]{1,0:T(8,128)S(1)}, f32[32,16384]{1,0:T(8,128)}, u32[]{:S(2)}) copy-start(f32[32,16384]{1,0:T(8,128)} %x_ref.1) | copy-start | bytes 6291460
  1.6 0.9 %copy-start.1 = (f32[32,2048]{1,0:T(8,128)S(1)}, f32[32,2048]{1,0:T(8,128)}, u32[]{:S(2)}) copy-start(f32[32,2048]{1,0:T(8,128)} %y_ref.1) | copy-start | bytes 786436
  2.5 0.7 copy-start.2
  3.2 0.7 copy-start.3

commit v4 on v3

--- a/solution.py
+++ b/solution.py
@@ -19,7 +19,7 @@
 
 
 chunks = 2
-delay = 4
+delay = 3
 
 
 def fused_kernel(

time: 93 us -> 95.1 us (1.023)
  Pallas kernels: 88.3 us -> 90.4 us
    pallas_call x1, Pallas kernels: 76.7 us -> 78.8 us  [fused(): pl.pallas_call(functools.partial(fused_kernel, n_t, n_q), out_shape=jax.S...]
where the time goes in v4:
time: 95.1 us; the launch traced here: 94.9 us
  Pallas kernels  90.4 us (95%)
  local copies, waits for them, and re-layouts  4.48 us (5%)
    pallas_call x1, Pallas kernels, fused(): pl.pallas_call(functools.partial(fused_kernel, n_t, n_q), out_shape=jax.S...  78.8 us
    pallas_call x1, Pallas kernels, scatter(): pl.pallas_call(functools.partial(scatter_kernel, n_t), out_shape=jax.Shap...  11.6 us
    unnamed x9, local copies, waits for them, and re-layouts  4.48 us

profile of v4, /device:TPU:0, one launch (start us, length us, event | category | flops | bytes accessed | tf_op | source)
XLA Modules:
  0.0 94.9 jit_solution(1601947578854996143)
XLA Ops:
  0.0 0.0 copy-start
  0.0 1.6 %copy-done = f32[32,16384]{1,0:T(8,128)S(1)} copy-done((f32[32,16384]{1,0:T(8,128)S(1)}, f32[32,16384]{1,0:T(8,128)}, u32[]{:S(2)}) %copy-start) | copy-done | bytes 2097176
  1.6 0.0 copy-start.1
  1.6 0.9 copy-done.1
  2.5 0.0 copy-start.2
  2.5 0.7 copy-done.2
  3.2 0.0 copy-start.3
  3.2 0.7 copy-done.3
  3.9 78.8 %shard_map.46 = f32[64,2048]{1,0:T(8,128)S(1)} custom-call(f32[32,16384]{1,0:T(8,128)S(1)} %copy-done, f32[32,2048]{1,0:T(8,128)S(1)} %copy-done.1, s32[1,32]{1,0:T(1,128)S(1)} %bitcast.4, s32[1,64]{1,0:T(1,128)S(1)} %bitcast.5), custom_call_target="tpu_custom_call" | custom-call | tf_op jit(solution)/shard_map/pallas_call | solution.py:302
  82.6 11.6 %shard_map.47 = f32[8,2048]{1,0:T(8,128)S(1)} custom-call(f32[4,2,8,2048]{3,2,1,0:T(8,128)S(1)} %bitcast.3), custom_call_target="tpu_custom_call" | custom-call | tf_op jit(solution)/shard_map/pallas_call | solution.py:374
  94.3 0.6 copy.6
Async XLA Ops:
  0.0 1.6 %copy-start = (f32[32,16384]{1,0:T(8,128)S(1)}, f32[32,16384]{1,0:T(8,128)}, u32[]{:S(2)}) copy-start(f32[32,16384]{1,0:T(8,128)} %x_ref.1) | copy-start | bytes 6291460
  1.6 0.9 %copy-start.1 = (f32[32,2048]{1,0:T(8,128)S(1)}, f32[32,2048]{1,0:T(8,128)}, u32[]{:S(2)}) copy-start(f32[32,2048]{1,0:T(8,128)} %y_ref.1) | copy-start | bytes 786436
  2.5 0.7 copy-start.2
  3.2 0.7 copy-start.3
